TPU v7x, 32 devices: a whole 2x2x4 slice. The times are simulated.
32 devices in a mesh: fsdp: 16 (over z, y, x), tp: 2 (over core).
Axes of the slice: x: 2, y: 2, z: 4, core: 2. Of those that a mesh axis runs over, the one named last changes fastest.
Arguments:
- owner: int32 [2, 7], replicated, may hold values from 0 to 15, as said below
- grads: bfloat16 [2, 896, 2, 8320], P(None, 'fsdp', 'tp')
- weights: float32 [2, 896, 2, 8320], P(None, 'fsdp', 'tp'), may hold values from -0.1875 to 0.1875
- adam_m: float32 [2, 896, 2, 8320], P(None, 'fsdp', 'tp'), may hold values from -0.4375 to 0.4375
- adam_v: float32 [2, 896, 2, 8320], P(None, 'fsdp', 'tp'), may hold values from 0.0001 to 0.1
- stats: float32 [16, 896, 896], P('fsdp', 'tp')
- roots: bfloat16 [16, 896, 896], P('fsdp', 'tp')
- vec_weight: float32 [2, 2944], P(None, ('fsdp', 'tp')), may hold values from 0.5 to 1.5
- vec_grad: bfloat16 [2, 2944], P(None, ('fsdp', 'tp')), may hold values from -1.5 to 1.5
- vec_m: float32 [2, 2944], P(None, ('fsdp', 'tp')), may hold values from -0.4375 to 0.4375
- vec_v: float32 [2, 2944], P(None, ('fsdp', 'tp')), may hold values from 0.0001 to 0.1
Outputs:
- weights_new: float32 [2, 896, 2, 8320], P(None, 'fsdp', 'tp')
- adam_m_new: float32 [2, 896, 2, 8320], P(None, 'fsdp', 'tp')
- adam_v_new: float32 [2, 896, 2, 8320], P(None, 'fsdp', 'tp')
- stats_new: float32 [16, 896, 896], P('fsdp', 'tp')
- vec_weight_new: float32 [2, 2944], P(None, ('fsdp', 'tp'))
- vec_m_new: float32 [2, 2944], P(None, ('fsdp', 'tp'))
- vec_v_new: float32 [2, 2944], P(None, ('fsdp', 'tp'))
Inputs may be any that keep to these rules, and one draw needn't show every extreme that they name: owner[l, t] is the index along fsdp of the chip whose slot holds the statistic of kind t of layer l; all 14 values are distinct, so a chip owns at most one matrix and some chips own none.
All inputs are finite; a program needn't handle non-finite values.
Results may differ from a plain program's by a relative error of at most 0.0015.
Values may be sent and summed in bfloat16 or wider, within the bound.
No kernel may reach another device: no remote copies, remote signals or barrier semaphores. Data moves between devices by JAX's collectives and lax.ppermute only.
A program may use at most 192 MiB of HBM per device.

v0:
```python
import jax
import jax.numpy as jnp
from jax import lax
from jax.sharding import PartitionSpec as P

FF = 4864
QW = 896
KW = 128


def half_widths():
    return [QW // 2, KW // 2, KW // 2, QW // 2, FF // 2, FF // 2, FF // 2]


def column_starts(widths):
    starts = []
    position = 0
    for wide in widths:
        starts.append(position)
        position = position + wide
    return starts


def kind_sums(values, widths, starts):
    return jnp.stack(
        [
            jnp.sum(values[:, :, starts[kind] : starts[kind] + widths[kind]], axis=(1, 2))
            for kind in range(7)
        ],
        axis=1,
    )


def gram_rows(left, right):
    return lax.dot_general(
        left, right, (((1,), (1,)), ((), ())), preferred_element_type=jnp.float32
    )


def on_device(
    owner, grads, weights, adam_m, adam_v, stats, roots, vec_weight, vec_grad, vec_m, vec_v
):
    widths = half_widths()
    starts = column_starts(widths)
    classes = [widths[0], widths[1], widths[4]]
    class_table = jnp.array([0, 1, 1, 0, 2, 2, 2], jnp.int32)
    chips = lax.axis_size("fsdp")
    layers = grads.shape[0]
    rows = grads.shape[1]
    capacity = FF // 2
    model_rows = rows * chips
    local_grad = grads[:, :, 0, :]
    grad_float = grads.astype(jnp.float32)
    adam_m_new = 0.9 * adam_m + 0.1 * grad_float
    adam_v_new = 0.99 * adam_v + 0.01 * grad_float * grad_float
    adam_step = (adam_m_new / (jnp.sqrt(adam_v_new) + 1e-08))[:, :, 0, :]
    adam_part = kind_sums(adam_step * adam_step, widths, starts)
    adam_total = lax.psum(adam_part, ("fsdp", "tp"))
    outgoing = jnp.zeros((chips, rows, capacity), jnp.bfloat16)
    for kind in range(7):
        outgoing = outgoing.at[owner[:, kind], :, : widths[kind]].set(
            local_grad[:, :, starts[kind] : starts[kind] + widths[kind]]
        )
    arrived = lax.all_to_all(outgoing, "fsdp", split_axis=0, concat_axis=0, tiled=True)
    gathered = arrived.reshape(model_rows, capacity)
    chip_index = lax.axis_index("fsdp")
    matches = owner == chip_index
    owned = jnp.any(matches)
    width_class = jnp.where(owned, jnp.sum(jnp.where(matches, class_table[None, :], 0)), 1)
    stat_slot = stats[0]
    root_slot = roots[0]

    def stat_term_rows():

        def make_rows(wide):

            def branch():
                block = gathered[:, :wide]
                return gram_rows(block, gathered[:, :wide])

            return branch

        return lax.switch(width_class, [make_rows(wide) for wide in classes])

    stat_term = lax.psum_scatter(stat_term_rows(), "tp", scatter_dimension=0, tiled=True)

    def apply_rows(piece):

        def make_apply(wide):

            def branch():
                result = jnp.dot(piece, gathered[:, :wide], preferred_element_type=jnp.float32)
                return jnp.pad(result, ((0, 0), (0, capacity - wide)))

            return branch

        return lax.switch(width_class, [make_apply(wide) for wide in classes])

    precond = apply_rows(lax.all_gather(root_slot, "tp", axis=0, tiled=True)).astype(jnp.bfloat16)
    stats_new = jnp.where(owned, 0.9 * stat_slot + 0.1 * stat_term, stat_slot)[None]
    returned = lax.all_to_all(
        precond.reshape(chips, rows, capacity), "fsdp", split_axis=0, concat_axis=0, tiled=True
    )
    pieces = [returned[owner[:, kind], :, : widths[kind]] for kind in range(7)]
    direction = jnp.concatenate(pieces, axis=2).astype(jnp.float32)
    shampoo_part = kind_sums(direction * direction, widths, starts)
    shampoo_total = lax.psum(shampoo_part, ("fsdp", "tp"))
    ratio = jnp.sqrt(adam_total) / (jnp.sqrt(shampoo_total) + 1e-06)
    column_scale = jnp.concatenate(
        [jnp.broadcast_to(ratio[:, kind : kind + 1], (layers, widths[kind])) for kind in range(7)],
        axis=1,
    )
    weights_new = weights - 0.02 * (direction * column_scale[:, None, :])[:, :, None, :]
    vec_float = vec_grad.astype(jnp.float32)
    vec_m_new = 0.9 * vec_m + 0.1 * vec_float
    vec_v_new = 0.99 * vec_v + 0.01 * vec_float * vec_float
    vec_weight_new = vec_weight - 0.02 * vec_m_new / (jnp.sqrt(vec_v_new) + 1e-08)
    return (weights_new, adam_m_new, adam_v_new, stats_new, vec_weight_new, vec_m_new, vec_v_new)


def solution(mesh):
    placed = (
        P(),
        P(None, "fsdp", "tp", None),
        P(None, "fsdp", "tp", None),
        P(None, "fsdp", "tp", None),
        P(None, "fsdp", "tp", None),
        P("fsdp", "tp", None),
        P("fsdp", "tp", None),
        P(None, ("fsdp", "tp")),
        P(None, ("fsdp", "tp")),
        P(None, ("fsdp", "tp")),
        P(None, ("fsdp", "tp")),
    )
    return jax.shard_map(
        on_device,
        mesh=mesh,
        in_specs=placed,
        out_specs=(
            P(None, "fsdp", "tp", None),
            P(None, "fsdp", "tp", None),
            P(None, "fsdp", "tp", None),
            P("fsdp", "tp", None),
            P(None, ("fsdp", "tp")),
            P(None, ("fsdp", "tp")),
            P(None, ("fsdp", "tp")),
        ),
        check_vma=False,
    )
```

profile of v0, /device:TPU:0, one launch (start us, length us, event | category | flops | bytes accessed | tf_op | source)
XLA Modules:
  0.0 411.3 jit_solution(16580479824753953919)
XLA Ops:
  13.3 16.8 %while.4 = (s32[]{:T(128)}, bf16[16,56,2432]{2,1,0:T(8,128)(2,1)}, s32[2,2]{1,0:T(2,128)S(1)}, bf16[2,56,448]{2,1,0:T(8,128)(2,1)S(1)}, s32[]{:T(128)}, /*index=5*/s32[3]{0:T(128)S(1)}, s32[1]{0:T(128)}, s32[]{:T(128)}) while((s32[]{:T(128)}, bf16[16,56,2432]{2,1,0:T(8,128)(2,1)}, s32[2,2]{1,0:T(2,128)S(1)}, bf16[2,56,448]{2,1,0:T(8,128)(2,1)S(1)}, ...), condition=%wide.while_cond, body=%wide.while_body.sunk | while | flops 25107 | bytes 251051 | solution.py:61
  15.9 2.9 dynamic-slice_select_fusion.8
  24.3 2.9 dynamic-slice_select_fusion.8
  27.2 2.9 dynamic-update-slice.12
  30.1 16.1 %while.5 = (s32[]{:T(128)}, bf16[16,56,2432]{2,1,0:T(8,128)(2,1)}, s32[2,2]{1,0:T(2,128)S(1)}, bf16[2,56,64]{2,1,0:T(8,128)(2,1)S(1)}, s32[]{:T(128)}, /*index=5*/s32[3]{0:T(128)S(1)}, s32[1]{0:T(128)}, s32[]{:T(128)}) while((s32[]{:T(128)}, bf16[16,56,2432]{2,1,0:T(8,128)(2,1)}, s32[2,2]{1,0:T(2,128)S(1)}, bf16[2,56,64]{2,1,0:T(8,128)(2,1)S(1)}, ...), condition=%wide.while_cond.1, body=%wide.while_body.1.sunk | while | flops 3603 | bytes 36011 | solution.py:61
  46.2 16.1 %while.6 = (s32[]{:T(128)}, bf16[16,56,2432]{2,1,0:T(8,128)(2,1)}, s32[2,2]{1,0:T(2,128)S(1)}, bf16[2,56,64]{2,1,0:T(8,128)(2,1)S(1)}, s32[]{:T(128)}, /*index=5*/s32[3]{0:T(128)S(1)}, s32[1]{0:T(128)}, s32[]{:T(128)}) while((s32[]{:T(128)}, bf16[16,56,2432]{2,1,0:T(8,128)(2,1)}, s32[2,2]{1,0:T(2,128)S(1)}, bf16[2,56,64]{2,1,0:T(8,128)(2,1)S(1)}, ...), condition=%wide.while_cond.2, body=%wide.while_body.2.sunk | while | flops 3603 | bytes 36011 | solution.py:61
  62.3 16.7 %while.7 = (s32[]{:T(128)}, bf16[16,56,2432]{2,1,0:T(8,128)(2,1)}, s32[2,2]{1,0:T(2,128)S(1)}, bf16[2,56,448]{2,1,0:T(8,128)(2,1)S(1)}, s32[]{:T(128)}, /*index=5*/s32[3]{0:T(128)S(1)}, s32[1]{0:T(128)}, s32[]{:T(128)}) while((s32[]{:T(128)}, bf16[16,56,2432]{2,1,0:T(8,128)(2,1)}, s32[2,2]{1,0:T(2,128)S(1)}, bf16[2,56,448]{2,1,0:T(8,128)(2,1)S(1)}, ...), condition=%wide.while_cond.3, body=%wide.while_body.3.sunk | while | flops 25107 | bytes 251051 | solution.py:61
  64.9 2.9 dynamic-slice_select_fusion.11
  73.2 2.9 dynamic-slice_select_fusion.11
  86.3 8.5 %all-to-all-start = ((bf16[16,56,2432]{2,1,0:T(8,128)(2,1)}), bf16[16,56,2432]{2,1,0:T(8,128)(2,1)}, u32[]{:S(2)}, u32[]{:S(2)}) async-start(bf16[16,56,2432]{2,1,0:T(8,128)(2,1)} %scatter_fusion.2), calls=%async_computation | async-start | bytes 8716288 | tf_op jit(solution)/shard_map/all_to_all | solution.py:64
  98.0 10.3 %all-gather.3.cloned.1.call-done = bf16[1,896,896]{2,1,0:T(8,128)(2,1)} async-done(((bf16[1,448,896]{2,1,0:T(8,128)(2,1)}), bf16[1,896,896]{2,1,0:T(8,128)(2,1)}) %all-gather.3.cloned.1.call-update) | async-done | bytes 1605648 | tf_op jit(solution)/shard_map/all_gather | solution.py:99
  108.3 69.2 %all-to-all-done = bf16[16,56,2432]{2,1,0:T(8,128)(2,1)} async-done(((bf16[16,56,2432]{2,1,0:T(8,128)(2,1)}), bf16[16,56,2432]{2,1,0:T(8,128)(2,1)}, u32[]{:S(2)}, u32[]{:S(2)}) %all-to-all-start) | async-done | bytes 4358176 | tf_op jit(solution)/shard_map/all_to_all | solution.py:64
  177.5 5.1 %conditional.2 = (bf16[896,2432]{0,1:T(8,128)(2,1)}) conditional(s32[]{:T(128)} %clamp.4, (bf16[896,2432]{1,0:T(8,128)(2,1)}, bf16[896,896]{1,0:T(8,128)(2,1)}) %tuple.144, (bf16[896,2432]{1,0:T(8,128)(2,1)}, bf16[896,896]{1,0:T(8,128)(2,1)}) %tuple.145, (bf16[896,896]{1,0:T(8,128)(2,1)}, bf16[896,2432]{1,0:T(8,128)(2,1)}) %tuple.146), branch_computations={%region_9.0_spmd, %region_10.0_spmd, %region_11.0_spmd} | conditional | flops 3904897024 | bytes 10321928 | solution.py:97
  182.7 7.1 %copy.72 = bf16[896,2432]{1,0:T(8,128)(2,1)} copy(bf16[896,2432]{0,1:T(8,128)(2,1)} %get-tuple-element.397) | data formatting | bytes 8716288 | tf_op jit(solution)/shard_map/cond | solution.py:97
  189.8 25.4 %all-to-all-start.1 = ((bf16[16,56,2432]{2,1,0:T(8,128)(2,1)}), bf16[16,56,2432]{2,1,0:T(8,128)(2,1)}, u32[]{:S(2)}, u32[]{:S(2)}) async-start(bf16[16,56,2432]{2,1,0:T(8,128)(2,1)} %bitcast.96), calls=%async_computation.1 | async-start | bytes 8716288 | tf_op jit(solution)/shard_map/all_to_all | solution.py:101
  215.2 4.5 %conditional.3 = (f32[896,896]{1,0:T(8,128)}) conditional(s32[]{:T(128)} %clamp.4, bf16[896,2432]{1,0:T(8,128)(2,1)} %bitcast.1, bf16[896,2432]{1,0:T(8,128)(2,1)} %bitcast.1, bf16[896,2432]{1,0:T(8,128)(2,1)} %bitcast.1), branch_computations={%region_28.29_spmd, %region_29.30_spmd, %region_30.31_spmd} | conditional | flops 3904897024 | bytes 7569416 | solution.py:83
  215.4 4.4 %fusion.4 = f32[896,896]{1,0:T(8,128)} fusion(bf16[896,2432]{1,0:T(8,128)(2,1)} %param.3), kind=kOutput, calls=%fused_computation.14 | convolution fusion | flops 719323136 | bytes 4128768 | tf_op jit(solution)/shard_map/cond/branch_0_fun/dot_general | solution.py:35
  221.3 20.8 %divide_multiply_fusion = (f32[2,56,1,8320]{3,2,1,0:T(1,128)S(1)}, f32[2,56,1,8320]{3,2,1,0:T(1,128)}, f32[2,56,1,8320]{3,2,1,0:T(1,128)}) fusion(bf16[2,56,1,8320]{3,1,2,0:T(8,128)(2,1)S(1)} %copy-done.1, f32[2,56,1,8320]{3,2,1,0:T(1,128)} %param.22, f32[2,56,1,8320]{3,2,1,0:T(1,128)} %param.21), kind=kLoop, calls=%fused_computation.36 | loop fusion | flops 10250240 | bytes 20500480 | tf_op jit(solution)/shard_map/mul | solution.py:57
  249.4 3.4 fusion.10
  252.7 43.8 %all-to-all-done.1 = bf16[16,56,2432]{2,1,0:T(8,128)(2,1)} async-done(((bf16[16,56,2432]{2,1,0:T(8,128)(2,1)}), bf16[16,56,2432]{2,1,0:T(8,128)(2,1)}, u32[]{:S(2)}, u32[]{:S(2)}) %all-to-all-start.1) | async-done | bytes 4358176 | tf_op jit(solution)/shard_map/all_to_all | solution.py:101
  296.5 12.8 %copy.73 = bf16[16,56,2432]{1,0,2:T(8,128)(2,1)} copy(bf16[16,56,2432]{2,1,0:T(8,128)(2,1)} %all-to-all-done.1) | data formatting | bytes 8716288 | tf_op jit(solution)/shard_map/all_to_all | solution.py:101
  314.3 3.1 gather_fusion.3
  337.4 55.1 %all-reduce.6 = (f32[2,7]{1,0:T(2,128)S(1)}, f32[2,7]{1,0:T(2,128)S(1)}) all-reduce(f32[2,7]{1,0:T(2,128)S(1)} %stack.63, f32[2,7]{1,0:T(2,128)S(1)} %stack.55), channel_id=1, replica_groups=mesh['fsdp'=16,'tp'=2] {'fsdp','tp'}, use_global_device_ids=true, to_apply=%region_27.28 | all-reduce | flops 28 | bytes 224 | tf_op jit(solution)/shard_map/psum | solution.py:107
  398.8 5.7 %copy.101 = f32[2,56,1,8320]{3,2,1,0:T(1,128)} copy(f32[2,56,1,8320]{3,1,0,2:T(8,128)S(1)} %copy_subtract_fusion) | data formatting | bytes 7454720
  (144 shorter events, 111.4 us)
Async XLA Ops:
  7.2 3.5 copy-start.9
  9.1 4.2 %copy-start.10 = (s32[3]{0:T(128)S(1)}, s32[3]{0:T(128)}, u32[]{:S(2)}) copy-start(s32[3]{0:T(128)} %constant.291) | copy-start | bytes 40
  10.6 19.5 %copy-start.11 = (s32[3]{0:T(128)S(1)}, s32[3]{0:T(128)}, u32[]{:S(2)}) copy-start(s32[3]{0:T(128)} %constant.305) | copy-start | bytes 40
  86.3 9.9 %copy-start.15 = (s32[7]{0:T(128)S(1)}, s32[7]{0:T(128)}, u32[]{:S(2)}) copy-start(s32[7]{0:T(128)} %constant.14.clone) | copy-start | bytes 88
  86.3 91.2 %all-to-all-start = ((bf16[16,56,2432]{2,1,0:T(8,128)(2,1)}), bf16[16,56,2432]{2,1,0:T(8,128)(2,1)}, u32[]{:S(2)}, u32[]{:S(2)}) async-start(bf16[16,56,2432]{2,1,0:T(8,128)(2,1)} %scatter_fusion.2), calls=%async_computation | async-start | bytes 8716288 | tf_op jit(solution)/shard_map/all_to_all | solution.py:64
  94.8 13.5 %all-gather.3.cloned.1.call-start = ((), (), s32[]{:S(2)}) async-start(), calls=%async_computation.4 | async-start | bytes 2408448 | tf_op jit(solution)/shard_map/all_gather | solution.py:99
  189.8 106.8 %all-to-all-start.1 = ((bf16[16,56,2432]{2,1,0:T(8,128)(2,1)}), bf16[16,56,2432]{2,1,0:T(8,128)(2,1)}, u32[]{:S(2)}, u32[]{:S(2)}) async-start(bf16[16,56,2432]{2,1,0:T(8,128)(2,1)} %bitcast.96), calls=%async_computation.1 | async-start | bytes 8716288 | tf_op jit(solution)/shard_map/all_to_all | solution.py:101
  215.2 34.2 %reduce-scatter.2.cloned.1.call-start = ((), (), s32[]{:S(2)}) async-start(), calls=%async_computation.3 | async-start | bytes 4816896 | tf_op jit(solution)/shard_map/reduce_scatter | solution.py:85
  219.8 1.5 copy-start.1
  242.4 1.9 copy-start
  242.4 6.3 %copy-start.12 = (f32[2,92]{1,0:T(2,128)S(1)}, f32[2,92]{1,0:T(2,128)}, u32[]{:S(2)}) copy-start(f32[2,92]{1,0:T(2,128)} %param.25) | copy-start | bytes 2212
  242.4 6.3 %copy-start.13 = (f32[2,92]{1,0:T(2,128)S(1)}, f32[2,92]{1,0:T(2,128)}, u32[]{:S(2)}) copy-start(f32[2,92]{1,0:T(2,128)} %param.27) | copy-start | bytes 2212
  242.4 6.3 %copy-start.14 = (f32[2,92]{1,0:T(2,128)S(1)}, f32[2,92]{1,0:T(2,128)}, u32[]{:S(2)}) copy-start(f32[2,92]{1,0:T(2,128)} %param.28) | copy-start | bytes 2212
  242.4 6.3 %copy-start.16 = (bf16[2,92]{1,0:T(2,128)(2,1)S(1)}, bf16[2,92]{1,0:T(2,128)(2,1)}, u32[]{:S(2)}) copy-start(bf16[2,92]{1,0:T(2,128)(2,1)} %param.26) | copy-start | bytes 1108
  242.5 6.9 %copy-start.2 = (f32[1,448,896]{2,1,0:T(8,128)S(1)}, f32[1,448,896]{2,1,0:T(8,128)}, u32[]{:S(2)}) copy-start(f32[1,448,896]{2,1,0:T(8,128)} %param.23) | copy-start | bytes 4816900
  313.6 3.8 copy-start.7
  317.4 10.2 %copy-start.5 = (bf16[2,56,448]{1,0,2:T(2,128)(2,1)}, bf16[2,56,448]{1,0,2:T(2,128)(2,1)S(1)}, u32[]{:S(2)}) copy-start(bf16[2,56,448]{1,0,2:T(2,128)(2,1)S(1)} %gather_fusion.3) | copy-start | bytes 301060
  320.3 7.3 %copy-start.3 = (bf16[2,56,448]{1,0,2:T(2,128)(2,1)}, bf16[2,56,448]{1,0,2:T(2,128)(2,1)S(1)}, u32[]{:S(2)}) copy-start(bf16[2,56,448]{1,0,2:T(2,128)(2,1)S(1)} %gather_fusion) | copy-start | bytes 301060
  333.6 1.5 copy-start.8
  333.6 1.6 copy-start.6
  333.6 3.1 copy-start.4
Sparse Core Ops, SparseCore 0:
  97.2 11.0 all-gather.2
  219.9 17.0 reduce-scatter.1
where the time goes:
time: 415 us; the launch traced here: 411 us
  waiting for transfers between devices  124 us (30%)
  local copies, waits for them, and re-layouts  103 us (25%)
  other arithmetic  72.3 us (17%)
  blocking collectives  55.1 us (13%)
  starting transfers between devices  34 us (8%)
  between operations  15.6 us (4%)
  matrix products  7.14 us (2%)
    all_to_all x1, waiting for transfers between devices, on_device(): lax.all_to_all(outgoing, 'fsdp', split_axis=0, concat_axis=0, tiled=True)  69.2 us
    psum x1, blocking collectives, on_device(): shampoo_total = lax.psum(shampoo_part, ('fsdp', 'tp'))  55.1 us
    all_to_all x1, waiting for transfers between devices, on_device(): lax.all_to_all(precond.reshape(chips, rows, capacity), 'fsdp', split_axis...  43.8 us
    scatter x16, other arithmetic  38.8 us
    scatter x24, local copies, waits for them, and re-layouts  26.9 us
    all_to_all x1, starting transfers between devices, on_device(): lax.all_to_all(precond.reshape(chips, rows, capacity), 'fsdp', split_axis...  25.4 us
    gather x11, local copies, waits for them, and re-layouts, on_device(): pieces = [returned[owner[:, kind], :, :widths[kind]] for kind in range(7)]  21.1 us
    mul x1, other arithmetic, on_device(): adam_part = kind_sums(adam_step * adam_step, widths, starts)  20.8 us
  transfers between devices with their start and end apart: 4, of which 3 were waited for; matrix products, arithmetic and copies ran while one was open for 9% of the time, Pallas kernels for 0%

commit v1 on v0

--- a/solution.py
+++ b/solution.py
@@ -104,7 +104,8 @@
     pieces = [returned[owner[:, kind], :, : widths[kind]] for kind in range(7)]
     direction = jnp.concatenate(pieces, axis=2).astype(jnp.float32)
     shampoo_part = kind_sums(direction * direction, widths, starts)
-    shampoo_total = lax.psum(shampoo_part, ("fsdp", "tp"))
+    parts = lax.all_gather(shampoo_part, ("fsdp", "tp"), axis=0, tiled=False)
+    shampoo_total = parts.sum(axis=0)
     ratio = jnp.sqrt(adam_total) / (jnp.sqrt(shampoo_total) + 1e-06)
     column_scale = jnp.concatenate(
         [jnp.broadcast_to(ratio[:, kind : kind + 1], (layers, widths[kind])) for kind in range(7)],

time: 415 us -> 440 us (1.060)
  blocking collectives: 55.1 us -> 124 us
  waiting for transfers between devices: 124 us -> 80.2 us
    all_to_all x1, waiting for transfers between devices: 43.8 us -> 0.01 us  [on_device(): lax.all_to_all(precond.reshape(chips, rows, capacity), 'fsdp', split_axis...]
    all_gather x0 -> x1, blocking collectives: none -> 41.1 us  [on_device(): parts = lax.all_gather(shampoo_part, ('fsdp', 'tp'), axis=0, tiled=False)]
    psum x1, blocking collectives: 55.1 us -> 82.8 us  [on_device(): adam_total = lax.psum(adam_part, ('fsdp', 'tp'))]
  transfers between devices with their start and end apart: 4 -> 4, of which waited for: 3 -> 2; matrix products, arithmetic and copies ran while one was open for 9% -> 8% of each run, Pallas kernels for 0% -> 0%
where the time goes in v1:
time: 440 us; the launch traced here: 436 us
  blocking collectives  124 us (28%)
  local copies, waits for them, and re-layouts  103 us (23%)
  waiting for transfers between devices  80.2 us (18%)
  other arithmetic  72.4 us (16%)
  starting transfers between devices  34 us (8%)
  between operations  15.6 us (4%)
  matrix products  7.14 us (2%)
    psum x1, blocking collectives, on_device(): adam_total = lax.psum(adam_part, ('fsdp', 'tp'))  82.8 us
    all_to_all x1, waiting for transfers between devices, on_device(): lax.all_to_all(outgoing, 'fsdp', split_axis=0, concat_axis=0, tiled=True)  69.2 us
    all_gather x1, blocking collectives, on_device(): parts = lax.all_gather(shampoo_part, ('fsdp', 'tp'), axis=0, tiled=False)  41.1 us
    scatter x16, other arithmetic  38.8 us
    scatter x24, local copies, waits for them, and re-layouts  26.9 us
    all_to_all x1, starting transfers between devices, on_device(): lax.all_to_all(precond.reshape(chips, rows, capacity), 'fsdp', split_axis...  25.4 us
    gather x11, local copies, waits for them, and re-layouts, on_device(): pieces = [returned[owner[:, kind], :, :widths[kind]] for kind in range(7)]  21.1 us
    mul x1, other arithmetic, on_device(): adam_part = kind_sums(adam_step * adam_step, widths, starts)  20.8 us
  transfers between devices with their start and end apart: 4, of which 2 were waited for; matrix products, arithmetic and copies ran while one was open for 8% of the time, Pallas kernels for 0%

profile of v1, /device:TPU:0, one launch (start us, length us, event | category | flops | bytes accessed | tf_op | source)
XLA Modules:
  0.0 436.4 jit_solution(182656982739101708)
XLA Ops:
  13.3 16.8 %while.4 = (s32[]{:T(128)}, bf16[16,56,2432]{2,1,0:T(8,128)(2,1)}, s32[2,2]{1,0:T(2,128)S(1)}, bf16[2,56,448]{2,1,0:T(8,128)(2,1)S(1)}, s32[]{:T(128)}, /*index=5*/s32[3]{0:T(128)S(1)}, s32[1]{0:T(128)}, s32[]{:T(128)}) while((s32[]{:T(128)}, bf16[16,56,2432]{2,1,0:T(8,128)(2,1)}, s32[2,2]{1,0:T(2,128)S(1)}, bf16[2,56,448]{2,1,0:T(8,128)(2,1)S(1)}, ...), condition=%wide.while_cond, body=%wide.while_body.sunk | while | flops 25107 | bytes 251051 | solution.py:61
  15.9 2.9 dynamic-slice_select_fusion.8
  24.3 2.9 dynamic-slice_select_fusion.8
  27.2 2.9 dynamic-update-slice.12
  30.1 16.1 %while.5 = (s32[]{:T(128)}, bf16[16,56,2432]{2,1,0:T(8,128)(2,1)}, s32[2,2]{1,0:T(2,128)S(1)}, bf16[2,56,64]{2,1,0:T(8,128)(2,1)S(1)}, s32[]{:T(128)}, /*index=5*/s32[3]{0:T(128)S(1)}, s32[1]{0:T(128)}, s32[]{:T(128)}) while((s32[]{:T(128)}, bf16[16,56,2432]{2,1,0:T(8,128)(2,1)}, s32[2,2]{1,0:T(2,128)S(1)}, bf16[2,56,64]{2,1,0:T(8,128)(2,1)S(1)}, ...), condition=%wide.while_cond.1, body=%wide.while_body.1.sunk | while | flops 3603 | bytes 36011 | solution.py:61
  46.2 16.1 %while.6 = (s32[]{:T(128)}, bf16[16,56,2432]{2,1,0:T(8,128)(2,1)}, s32[2,2]{1,0:T(2,128)S(1)}, bf16[2,56,64]{2,1,0:T(8,128)(2,1)S(1)}, s32[]{:T(128)}, /*index=5*/s32[3]{0:T(128)S(1)}, s32[1]{0:T(128)}, s32[]{:T(128)}) while((s32[]{:T(128)}, bf16[16,56,2432]{2,1,0:T(8,128)(2,1)}, s32[2,2]{1,0:T(2,128)S(1)}, bf16[2,56,64]{2,1,0:T(8,128)(2,1)S(1)}, ...), condition=%wide.while_cond.2, body=%wide.while_body.2.sunk | while | flops 3603 | bytes 36011 | solution.py:61
  62.3 16.7 %while.7 = (s32[]{:T(128)}, bf16[16,56,2432]{2,1,0:T(8,128)(2,1)}, s32[2,2]{1,0:T(2,128)S(1)}, bf16[2,56,448]{2,1,0:T(8,128)(2,1)S(1)}, s32[]{:T(128)}, /*index=5*/s32[3]{0:T(128)S(1)}, s32[1]{0:T(128)}, s32[]{:T(128)}) while((s32[]{:T(128)}, bf16[16,56,2432]{2,1,0:T(8,128)(2,1)}, s32[2,2]{1,0:T(2,128)S(1)}, bf16[2,56,448]{2,1,0:T(8,128)(2,1)S(1)}, ...), condition=%wide.while_cond.3, body=%wide.while_body.3.sunk | while | flops 25107 | bytes 251051 | solution.py:61
  64.9 2.9 dynamic-slice_select_fusion.11
  73.2 2.9 dynamic-slice_select_fusion.11
  86.3 8.5 %all-to-all-start = ((bf16[16,56,2432]{2,1,0:T(8,128)(2,1)}), bf16[16,56,2432]{2,1,0:T(8,128)(2,1)}, u32[]{:S(2)}, u32[]{:S(2)}) async-start(bf16[16,56,2432]{2,1,0:T(8,128)(2,1)} %scatter_fusion.2), calls=%async_computation | async-start | bytes 8716288 | tf_op jit(solution)/shard_map/all_to_all | solution.py:64
  98.0 10.3 %all-gather.5.cloned.1.call-done = bf16[1,896,896]{2,1,0:T(8,128)(2,1)} async-done(((bf16[1,448,896]{2,1,0:T(8,128)(2,1)}), bf16[1,896,896]{2,1,0:T(8,128)(2,1)}) %all-gather.5.cloned.1.call-update) | async-done | bytes 1605648 | tf_op jit(solution)/shard_map/all_gather | solution.py:99
  108.3 69.2 %all-to-all-done = bf16[16,56,2432]{2,1,0:T(8,128)(2,1)} async-done(((bf16[16,56,2432]{2,1,0:T(8,128)(2,1)}), bf16[16,56,2432]{2,1,0:T(8,128)(2,1)}, u32[]{:S(2)}, u32[]{:S(2)}) %all-to-all-start) | async-done | bytes 4358176 | tf_op jit(solution)/shard_map/all_to_all | solution.py:64
  177.5 5.1 %conditional.2 = (bf16[896,2432]{0,1:T(8,128)(2,1)}) conditional(s32[]{:T(128)} %clamp.4, (bf16[896,2432]{1,0:T(8,128)(2,1)}, bf16[896,896]{1,0:T(8,128)(2,1)}) %tuple.144, (bf16[896,2432]{1,0:T(8,128)(2,1)}, bf16[896,896]{1,0:T(8,128)(2,1)}) %tuple.145, (bf16[896,896]{1,0:T(8,128)(2,1)}, bf16[896,2432]{1,0:T(8,128)(2,1)}) %tuple.146), branch_computations={%region_9.0_spmd, %region_10.0_spmd, %region_11.0_spmd} | conditional | flops 3904897024 | bytes 10321928 | solution.py:97
  182.7 7.1 %copy.74 = bf16[896,2432]{1,0:T(8,128)(2,1)} copy(bf16[896,2432]{0,1:T(8,128)(2,1)} %get-tuple-element.395) | data formatting | bytes 8716288 | tf_op jit(solution)/shard_map/cond | solution.py:97
  189.8 25.4 %all-to-all-start.1 = ((bf16[16,56,2432]{2,1,0:T(8,128)(2,1)}), bf16[16,56,2432]{2,1,0:T(8,128)(2,1)}, u32[]{:S(2)}, u32[]{:S(2)}) async-start(bf16[16,56,2432]{2,1,0:T(8,128)(2,1)} %bitcast.97), calls=%async_computation.1 | async-start | bytes 8716288 | tf_op jit(solution)/shard_map/all_to_all | solution.py:101
  215.2 4.5 %conditional.3 = (f32[896,896]{1,0:T(8,128)}) conditional(s32[]{:T(128)} %clamp.4, bf16[896,2432]{1,0:T(8,128)(2,1)} %bitcast.1, bf16[896,2432]{1,0:T(8,128)(2,1)} %bitcast.1, bf16[896,2432]{1,0:T(8,128)(2,1)} %bitcast.1), branch_computations={%region_28.29_spmd, %region_29.30_spmd, %region_30.31_spmd} | conditional | flops 3904897024 | bytes 7569416 | solution.py:83
  215.4 4.4 fusion.4
  221.3 20.8 %divide_multiply_fusion = (f32[2,56,1,8320]{3,2,1,0:T(1,128)S(1)}, f32[2,56,1,8320]{3,2,1,0:T(1,128)}, f32[2,56,1,8320]{3,2,1,0:T(1,128)}) fusion(bf16[2,56,1,8320]{3,1,2,0:T(8,128)(2,1)S(1)} %copy-done.1, f32[2,56,1,8320]{3,2,1,0:T(1,128)} %param.22, f32[2,56,1,8320]{3,2,1,0:T(1,128)} %param.21), kind=kLoop, calls=%fused_computation.36 | loop fusion | flops 10250240 | bytes 20500480 | tf_op jit(solution)/shard_map/mul | solution.py:57
  248.7 82.8 %psum.7 = f32[2,7]{1,0:T(2,128)S(1)} all-reduce(f32[2,7]{1,0:T(2,128)S(1)} %stack.55), channel_id=1, replica_groups=mesh['fsdp'=16,'tp'=2] {'fsdp','tp'}, use_global_device_ids=true, to_apply=%region_19.20 | all-reduce | flops 14 | bytes 112 | tf_op jit(solution)/shard_map/psum | solution.py:58
  332.2 3.4 fusion.10
  335.6 12.8 %copy.75 = bf16[16,56,2432]{1,0,2:T(8,128)(2,1)} copy(bf16[16,56,2432]{2,1,0:T(8,128)(2,1)} %all-to-all-done.1) | data formatting | bytes 8716288 | tf_op jit(solution)/shard_map/all_to_all | solution.py:101
  353.3 3.1 gather_fusion.3
  376.5 41.1 %all-gather.2 = f32[32,2,7]{2,1,0:T(2,128)S(1)} all-gather(f32[1,2,7]{2,1,0:T(2,128)S(1)} %bitcast.114), channel_id=3, replica_groups=mesh['fsdp'=16,'tp'=2] {'fsdp','tp'}, dimensions={0}, use_global_device_ids=true | all-gather | bytes 1848 | tf_op jit(solution)/shard_map/all_gather | solution.py:107
  423.9 5.7 %copy.103 = f32[2,56,1,8320]{3,2,1,0:T(1,128)} copy(f32[2,56,1,8320]{3,1,0,2:T(8,128)S(1)} %copy_subtract_fusion) | data formatting | bytes 7454720
  (146 shorter events, 111.4 us)
Async XLA Ops:
  7.2 3.5 copy-start.9
  9.1 4.2 copy-start.10
  10.6 19.5 %copy-start.11 = (s32[3]{0:T(128)S(1)}, s32[3]{0:T(128)}, u32[]{:S(2)}) copy-start(s32[3]{0:T(128)} %constant.305) | copy-start | bytes 40
  86.3 9.9 %copy-start.15 = (s32[7]{0:T(128)S(1)}, s32[7]{0:T(128)}, u32[]{:S(2)}) copy-start(s32[7]{0:T(128)} %constant.14.clone) | copy-start | bytes 88
  86.3 91.2 %all-to-all-start = ((bf16[16,56,2432]{2,1,0:T(8,128)(2,1)}), bf16[16,56,2432]{2,1,0:T(8,128)(2,1)}, u32[]{:S(2)}, u32[]{:S(2)}) async-start(bf16[16,56,2432]{2,1,0:T(8,128)(2,1)} %scatter_fusion.2), calls=%async_computation | async-start | bytes 8716288 | tf_op jit(solution)/shard_map/all_to_all | solution.py:64
  94.8 13.5 %all-gather.5.cloned.1.call-start = ((), (), s32[]{:S(2)}) async-start(), calls=%async_computation.4 | async-start | bytes 2408448 | tf_op jit(solution)/shard_map/all_gather | solution.py:99
  189.8 145.8 %all-to-all-start.1 = ((bf16[16,56,2432]{2,1,0:T(8,128)(2,1)}), bf16[16,56,2432]{2,1,0:T(8,128)(2,1)}, u32[]{:S(2)}, u32[]{:S(2)}) async-start(bf16[16,56,2432]{2,1,0:T(8,128)(2,1)} %bitcast.97), calls=%async_computation.1 | async-start | bytes 8716288 | tf_op jit(solution)/shard_map/all_to_all | solution.py:101
  215.2 117.0 %reduce-scatter.2.cloned.1.call-start = ((), (), s32[]{:S(2)}) async-start(), calls=%async_computation.3 | async-start | bytes 4816896 | tf_op jit(solution)/shard_map/reduce_scatter | solution.py:85
  219.8 1.5 copy-start.1
  242.4 1.9 copy-start
  242.4 89.2 %copy-start.12 = (f32[2,92]{1,0:T(2,128)S(1)}, f32[2,92]{1,0:T(2,128)}, u32[]{:S(2)}) copy-start(f32[2,92]{1,0:T(2,128)} %param.25) | copy-start | bytes 2212
  242.4 89.2 %copy-start.13 = (f32[2,92]{1,0:T(2,128)S(1)}, f32[2,92]{1,0:T(2,128)}, u32[]{:S(2)}) copy-start(f32[2,92]{1,0:T(2,128)} %param.27) | copy-start | bytes 2212
  242.4 89.2 %copy-start.14 = (f32[2,92]{1,0:T(2,128)S(1)}, f32[2,92]{1,0:T(2,128)}, u32[]{:S(2)}) copy-start(f32[2,92]{1,0:T(2,128)} %param.28) | copy-start | bytes 2212
  242.4 89.2 %copy-start.16 = (bf16[2,92]{1,0:T(2,128)(2,1)S(1)}, bf16[2,92]{1,0:T(2,128)(2,1)}, u32[]{:S(2)}) copy-start(bf16[2,92]{1,0:T(2,128)(2,1)} %param.26) | copy-start | bytes 1108
  242.5 89.7 %copy-start.2 = (f32[1,448,896]{2,1,0:T(8,128)S(1)}, f32[1,448,896]{2,1,0:T(8,128)}, u32[]{:S(2)}) copy-start(f32[1,448,896]{2,1,0:T(8,128)} %param.23) | copy-start | bytes 4816900
  352.6 0.7 copy-start.7
  356.4 10.2 %copy-start.3 = (bf16[2,56,448]{1,0,2:T(2,128)(2,1)}, bf16[2,56,448]{1,0,2:T(2,128)(2,1)S(1)}, u32[]{:S(2)}) copy-start(bf16[2,56,448]{1,0,2:T(2,128)(2,1)S(1)} %gather_fusion.3) | copy-start | bytes 301060
  359.3 7.3 %copy-start.5 = (bf16[2,56,448]{1,0,2:T(2,128)(2,1)}, bf16[2,56,448]{1,0,2:T(2,128)(2,1)S(1)}, u32[]{:S(2)}) copy-start(bf16[2,56,448]{1,0,2:T(2,128)(2,1)S(1)} %gather_fusion) | copy-start | bytes 301060
  372.6 1.5 copy-start.8
  372.6 1.6 copy-start.4
  372.6 2.3 copy-start.6
Sparse Core Ops, SparseCore 0:
  97.2 11.0 all-gather.4
  219.9 17.0 reduce-scatter.1
